TPU v7x, 256 devices: a whole 4x4x8 slice. The times are simulated.
256 devices in a mesh: pts: 32 (over x_hi, z, core), dir: 8 (over x_lo, y).
Axes of the slice: x: 4 (x_hi: 2, x_lo: 2; x = x_hi * 2 + x_lo), y: 4, z: 8, core: 2. Of those that a mesh axis runs over, the one named last changes fastest.
Arguments:
- action: float32 [50, 32, 512, 256], P(None, 'dir', 'pts'), may hold values from 0 to 60, as said below
- currents: float32 [2, 512, 256], P(None, 'pts'), may hold values from -0.1 to 0.1, as said below
- land_mask: int32 [512, 256], P('pts'), may hold values 0 or 1
- group_speed: float32 [50], replicated, may hold values from 0.02 to 0.55
- group_ratio: float32 [50], replicated, may hold values from 0.5 to 1
- bin_weight: float32 [50], replicated, may hold values from 0.002 to 0.02
Outputs:
- new_action: float32 [50, 32, 512, 256], P(None, 'dir', 'pts')
- wave_force: float32 [2, 512, 256], P(None, 'pts')
Inputs may be any that keep to these rules, and one draw needn't show every extreme that they name: Positive action densities. currents vary slowly from point to point.
All inputs are finite; a program needn't handle non-finite values. No bound on the sum of `land_mask` on one device may be relied on, other than what follows from the above.
Results may differ from a plain program's by a relative error of at most 0.00022.
Values sent between devices are 32-bit elements; how exact they have to be, the bound alone decides.
No kernel may reach another device: no remote copies, remote signals or barrier semaphores. Data moves between devices by JAX's collectives and lax.ppermute only.
A program may use at most 64 MiB of HBM per device.

v0:
```python
import math
import jax
import jax.numpy as jnp
from jax import lax
from jax.sharding import PartitionSpec as P


def with_halo(value, sides, width, wrap):
    for axis, dim in sides:
        count, length = (lax.axis_size(axis), value.shape[dim])
        up = [(i, (i + 1) % count) for i in range(count if wrap else count - 1)]
        down = [(j, i) for i, j in up]
        last = lax.slice_in_dim(value, length - width, length, axis=dim)
        first = lax.slice_in_dim(value, 0, width, axis=dim)
        before = lax.ppermute(last, axis, up)
        after = lax.ppermute(first, axis, down)
        value = jnp.concatenate([before, value, after], axis=dim)
    return value


def upwind(velocity, behind, in_front):
    return jnp.maximum(velocity, 0.0) * behind + jnp.minimum(velocity, 0.0) * in_front


def advance(extended, cur_u, cur_v, land_cells, cosine_terms, sine_terms, group_speed):
    speed_x = group_speed[:, None, None, None] * cosine_terms[None, :, None, None]
    speed_y = group_speed[:, None, None, None] * sine_terms[None, :, None, None]
    drift_x = speed_x + (0.5 * (cur_u[:-1] + cur_u[1:]))[None, None]
    flux_x = upwind(drift_x, extended[:, :, :-1], extended[:, :, 1:])
    middle = extended[:, :, 1:-1]
    side_v = jnp.pad(cur_v[1:-1], ((0, 0), (1, 1)))
    drift_y = speed_y + (0.5 * (side_v[:, :-1] + side_v[:, 1:]))[None, None]
    padded = jnp.pad(middle, ((0, 0), (0, 0), (0, 0), (1, 1)))
    flux_y = upwind(drift_y, padded[..., :-1], padded[..., 1:])
    change = flux_x[:, :, 1:] - flux_x[:, :, :-1] + (flux_y[..., 1:] - flux_y[..., :-1])
    return land_cells * (middle - change)


def row_slope(values):
    return 0.5 * (values[2:] - values[:-2])


def col_slope(values):
    padded = jnp.pad(values[1:-1], ((0, 0), (1, 1)))
    return 0.5 * (padded[:, 2:] - padded[:, :-2])


def shear_terms(ext_u, ext_v):
    return (row_slope(ext_u), col_slope(ext_u), row_slope(ext_v), col_slope(ext_v))


def turn_rate(face_angles, shears, total_dirs):
    u_dx, u_dy, v_dx, v_dy = shears
    sines = jnp.sin(face_angles)[:, None, None]
    cosines = jnp.cos(face_angles)[:, None, None]
    scale = total_dirs / (2.0 * math.pi)
    return scale * (
        sines * cosines * (u_dx - v_dy) + sines * sines * u_dy - cosines * cosines * v_dx
    )


def refract(cycle_ext, turning):
    flux = upwind(turning[None], cycle_ext[:, :-1], cycle_ext[:, 1:])
    return cycle_ext[:, 1:-1] - (flux[:, 1:] - flux[:, :-1])


def stress_table(angles, bin_weight, group_ratio):
    cos_sq = (jnp.cos(angles) * jnp.cos(angles))[None]
    sin_sq = (jnp.sin(angles) * jnp.sin(angles))[None]
    cross = (jnp.sin(angles) * jnp.cos(angles))[None]
    ratio = group_ratio[:, None]
    weight = bin_weight[:, None]
    return jnp.stack(
        [
            weight * (ratio * (1.0 + cos_sq) - 0.5),
            weight * ratio * cross,
            weight * (ratio * (1.0 + sin_sq) - 0.5),
        ]
    )


def wave_force_of(extended):
    first = -(row_slope(extended[0]) + col_slope(extended[1]))
    second = -(row_slope(extended[1]) + col_slope(extended[2]))
    return jnp.stack([first, second])


def per_device(action, currents, land_mask, group_speed, group_ratio, bin_weight):
    sector_count = action.shape[1]
    total_dirs = sector_count * lax.axis_size("dir")
    step_angle = 2.0 * math.pi / total_dirs
    offset = lax.axis_index("dir") * sector_count
    angles = (offset + jnp.arange(sector_count)).astype(jnp.float32) * step_angle
    cosine_terms = jnp.cos(angles)
    sine_terms = jnp.sin(angles)
    land_cells = land_mask.astype(jnp.float32)
    fields = jnp.stack([currents[0], currents[1], land_cells])
    beside_all = with_halo(fields, (("pts", 1),), 2, False)
    ext_u = beside_all[0, 1:-1]
    ext_v = beside_all[1, 1:-1]
    spectra = land_cells * action
    for substep in range(2):
        extended = with_halo(spectra, (("pts", 2),), 1, False)
        spectra = advance(extended, ext_u, ext_v, land_cells, cosine_terms, sine_terms, group_speed)
    shears = shear_terms(ext_u, ext_v)
    face_angles = ((offset + jnp.arange(sector_count + 1)).astype(jnp.float32) - 0.5) * step_angle
    turning = turn_rate(face_angles, shears, total_dirs)
    cycle_ext = with_halo(spectra, (("dir", 1),), 1, True)
    new_action = refract(cycle_ext, turning)
    partial_value = jnp.einsum(
        "kfd,fdry->kry",
        stress_table(angles, bin_weight, group_ratio),
        new_action,
        precision=lax.Precision.HIGHEST,
    )
    summed = lax.psum(partial_value, "dir")
    extended = with_halo(summed, (("pts", 1),), 1, False)
    return (new_action, wave_force_of(extended))


def solution(mesh):
    in_specs = (P(None, "dir", "pts", None), P(None, "pts", None), P("pts", None), P(), P(), P())
    out_specs = (P(None, "dir", "pts", None), P(None, "pts", None))
    return jax.shard_map(
        per_device, mesh=mesh, in_specs=in_specs, out_specs=out_specs, check_vma=False
    )
```

profile of v0, /device:TPU:6, one launch (start us, length us, event | category | flops | bytes accessed | tf_op | source)
XLA Modules:
  0.0 132.3 jit_solution(10773098734468614222)
XLA Ops:
  0.6 0.7 convert_bitcast_fusion
  1.4 0.7 pad_maximum_fusion.4
  2.1 1.9 %collective-permute-start = (f32[3,2,256]{2,1,0:T(2,128)S(1)}, f32[3,2,256]{2,1,0:T(2,128)S(1)}, u32[]{:S(2)}, u32[]{:S(2)}) collective-permute-start(f32[3,2,256]{2,1,0:T(2,128)S(1)} %get-tuple-element.24), channel_id=1, source_target_pairs={{0,8},{8,16},{16,24},{24,32},{32,40},{40,48},{48,56},{56,64},{64,7... | collective-permute-start | bytes 18440 | tf_op jit(solution)/shard_map/ppermute | solution.py:15
  4.0 8.0 %collective-permute-start.1 = (f32[3,2,256]{2,1,0:T(2,128)S(1)}, f32[3,2,256]{2,1,0:T(2,128)S(1)}, u32[]{:S(2)}, u32[]{:S(2)}) collective-permute-start(f32[3,2,256]{2,1,0:T(2,128)S(1)} %get-tuple-element.25), channel_id=1, source_target_pairs={{8,0},{16,8},{24,16},{32,24},{40,32},{48,40},{56,48},{64,56},{72,6... | collective-permute-start | bytes 18440 | tf_op jit(solution)/shard_map/ppermute | solution.py:16
  12.1 0.0 copy-start.5
  12.1 0.0 copy-start.6
  12.1 0.0 copy-start.7
  12.1 0.0 copy-start.4
  12.1 3.9 %copy_multiply_fusion = f32[50,4,16,256]{3,0,2,1:T(8,128)S(1)} fusion(f32[50,4,16,256]{3,2,1,0:T(8,128)} %param.6, f32[16,256]{1,0:T(8,128)S(1)} %get-tuple-element.30), kind=kLoop, calls=%fused_computation.35 | loop fusion | flops 819200 | bytes 6569984 | tf_op jit(solution)/shard_map/mul | solution.py:101
  16.0 1.8 %copy-done = f32[50,4,16,256]{3,0,2,1:T(8,128)} copy-done((f32[50,4,16,256]{3,0,2,1:T(8,128)}, f32[50,4,16,256]{3,0,2,1:T(8,128)S(1)}, u32[]{:S(2)}) %copy-start) | copy-done | bytes 3276824
  17.8 1.9 %collective-permute-start.2 = (f32[50,4,1,256]{3,0,2,1:T(8,128)S(1)}, f32[50,4,1,256]{3,0,2,1:T(8,128)S(1)}, u32[]{:S(2)}, u32[]{:S(2)}) collective-permute-start(f32[50,4,1,256]{3,0,2,1:T(8,128)S(1)} %get-tuple-element.15), channel_id=1, source_target_pairs={{0,8},{8,16},{16,24},{24,32},{32,40},{40,48},{48,56},{56,64},{64,7... | collective-permute-start | bytes 614408 | tf_op jit(solution)/shard_map/ppermute | solution.py:15
  19.7 7.3 %collective-permute-start.3 = (f32[50,4,1,256]{3,0,2,1:T(8,128)S(1)}, f32[50,4,1,256]{3,0,2,1:T(8,128)S(1)}, u32[]{:S(2)}, u32[]{:S(2)}) collective-permute-start(f32[50,4,1,256]{3,0,2,1:T(8,128)S(1)} %get-tuple-element.14), channel_id=1, source_target_pairs={{8,0},{16,8},{24,16},{32,24},{40,32},{48,40},{56,48},{64,56},{72,6... | collective-permute-start | bytes 614408 | tf_op jit(solution)/shard_map/ppermute | solution.py:16
  27.1 0.1 broadcast_multiply_fusion
  27.2 0.1 broadcast_multiply_fusion.2
  27.4 0.1 fusion.23
  27.4 4.8 %fusion.4 = f32[50,4,16,257]{3,0,2,1:T(8,128)S(1)} fusion(f32[50,4,16,256]{3,0,2,1:T(8,128)} %copy-done, f32[16,257]{1,0:T(8,128)S(1)} %fusion.23, f32[50,4]{0,1:T(4,128)S(1)} %get-tuple-element.34), kind=kLoop, calls=%fused_computation.12 | loop fusion | flops 4934400 | bytes 6583648 | tf_op jit(solution)/shard_map/add | solution.py:22
  32.3 0.0 copy-start.3
  32.3 1.2 fusion.11
  33.5 0.7 copy-done.3
  34.2 5.1 %fusion.19 = f32[50,4,16,256]{3,0,2,1:T(8,128)S(1)} fusion(f32[50,4,16,257]{3,0,2,1:T(8,128)S(1)} %fusion.4, f32[50,4,17,256]{3,0,2,1:T(8,128)S(1)} %fusion.11, f32[16,256]{1,0:T(8,128)S(1)} %get-tuple-element.30, f32[50,4,16,256]{3,2,1,0:T(8,128)S(1)} %copy-done.3), kind=kLoop, calls=%fused_computation.33 | loop fusion | flops 4915200 | bytes 19677184 | tf_op jit(solution)/shard_map/mul | solution.py:36
  39.4 1.9 %collective-permute-start.4 = (f32[50,4,1,256]{3,0,2,1:T(8,128)S(1)}, f32[50,4,1,256]{3,0,2,1:T(8,128)S(1)}, u32[]{:S(2)}, u32[]{:S(2)}) collective-permute-start(f32[50,4,1,256]{3,0,2,1:T(8,128)S(1)} %get-tuple-element.13), channel_id=1, source_target_pairs={{0,8},{8,16},{16,24},{24,32},{32,40},{40,48},{48,56},{56,64},{64,7... | collective-permute-start | bytes 614408 | tf_op jit(solution)/shard_map/ppermute | solution.py:15
  41.3 7.3 %collective-permute-start.5 = (f32[50,4,1,256]{3,0,2,1:T(8,128)S(1)}, f32[50,4,1,256]{3,0,2,1:T(8,128)S(1)}, u32[]{:S(2)}, u32[]{:S(2)}) collective-permute-start(f32[50,4,1,256]{3,0,2,1:T(8,128)S(1)} %get-tuple-element.12), channel_id=1, source_target_pairs={{8,0},{16,8},{24,16},{32,24},{40,32},{48,40},{56,48},{64,56},{72,6... | collective-permute-start | bytes 614408 | tf_op jit(solution)/shard_map/ppermute | solution.py:16
  48.6 3.3 %fusion.5 = f32[50,4,16,257]{3,0,2,1:T(8,128)} fusion(f32[50,4,16,256]{3,0,2,1:T(8,128)S(1)} %fusion.19, f32[16,257]{1,0:T(8,128)S(1)} %fusion.23, f32[50,4]{0,1:T(4,128)S(1)} %get-tuple-element.34), kind=kLoop, calls=%fused_computation.13 | loop fusion | flops 4934400 | bytes 6583648 | tf_op jit(solution)/shard_map/add | solution.py:22
  51.9 0.2 collective-permute-done.5
  52.1 2.5 %fusion.12 = f32[50,4,17,256]{3,0,2,1:T(8,128)} fusion(f32[50,4,16,256]{3,0,2,1:T(8,128)S(1)} %fusion.19, f32[50,4,1,256]{3,0,2,1:T(8,128)S(1)} %collective-permute-done.4, f32[50,4,1,256]{3,0,2,1:T(8,128)S(1)} %collective-permute-done.5, f32[17,256]{1,0:T(8,128)S(1)} %fusion.25, f32[50,4]{0,1:T(4,128)S(1)} %get-tuple-element.33), kind=kLoop, calls=%fused_computation.22 | loop fusion | flops 6963200 | bytes 7186208 | tf_op jit(solution)/shard_map/add | solution.py:22
  54.6 7.5 %fusion.16 = f32[50,4,16,256]{3,0,2,1:T(8,128)S(1)} fusion(f32[50,4,16,256]{3,0,2,1:T(8,128)S(1)} %fusion.19, f32[50,4,16,257]{3,0,2,1:T(8,128)} %fusion.5, f32[50,4,17,256]{3,0,2,1:T(8,128)} %fusion.12, f32[16,256]{1,0:T(8,128)S(1)} %get-tuple-element.30), kind=kLoop, calls=%fused_computation.28 | loop fusion | flops 4096000 | bytes 19677184 | tf_op jit(solution)/shard_map/mul | solution.py:36
  62.1 0.1 fusion.58
  62.2 0.3 copy.35
  62.5 1.7 %collective-permute-start.6 = (f32[50,1,16,256]{3,2,1,0:T(8,128)S(1)}, f32[50,1,16,256]{3,2,1,0:T(8,128)S(1)}, u32[]{:S(2)}, u32[]{:S(2)}) collective-permute-start(f32[50,1,16,256]{3,2,1,0:T(8,128)S(1)} %copy.35), channel_id=1, source_target_pairs={{0,1},{1,2},{2,3},{3,4},{4,5},{5,6},{6,7},{7,0},{8,9},{9,10},{10,1... | collective-permute-start | bytes 2457608 | tf_op jit(solution)/shard_map/ppermute | solution.py:15
  64.1 0.3 copy.37
  64.4 2.8 %collective-permute-start.7 = (f32[50,1,16,256]{3,2,1,0:T(8,128)S(1)}, f32[50,1,16,256]{3,2,1,0:T(8,128)S(1)}, u32[]{:S(2)}, u32[]{:S(2)}) collective-permute-start(f32[50,1,16,256]{3,2,1,0:T(8,128)S(1)} %copy.37), channel_id=1, source_target_pairs={{1,0},{2,1},{3,2},{4,3},{5,4},{6,5},{7,6},{0,7},{9,8},{10,9},{11,1... | collective-permute-start | bytes 2457608 | tf_op jit(solution)/shard_map/ppermute | solution.py:16
  67.3 0.1 add_multiply_fusion.1
  67.4 0.1 fusion.27
  67.5 0.1 fusion.21
  67.6 12.2 %collective-permute-done.6 = f32[50,1,16,256]{3,2,1,0:T(8,128)S(1)} collective-permute-done((f32[50,1,16,256]{3,2,1,0:T(8,128)S(1)}, f32[50,1,16,256]{3,2,1,0:T(8,128)S(1)}, u32[]{:S(2)}, u32[]{:S(2)}) %collective-permute-start.6) | collective-permute-done | bytes 819232 | tf_op jit(solution)/shard_map/ppermute | solution.py:15
  79.8 0.5 copy.36
  80.3 0.5 copy.38
  80.8 1.1 fusion.10
  81.9 0.6 fusion.13
  82.6 1.8 %copy-done.2 = f32[50,4,16,256]{3,0,2,1:T(8,128)} copy-done((f32[50,4,16,256]{3,0,2,1:T(8,128)}, f32[50,4,16,256]{3,0,2,1:T(8,128)S(1)}, u32[]{:S(2)}) %copy-start.2) | copy-done | bytes 3276824
  84.4 1.9 %convolution_bitcast_fusion = f32[3,16,256]{2,0,1:T(4,128)S(1)} fusion(f32[50,4,16,256]{3,0,2,1:T(8,128)S(1)} %fusion.13, f32[3,50,4]{1,2,0:T(4,128)S(1)} %pad_maximum_fusion.5), kind=kOutput, calls=%fused_computation.36 | convolution fusion | flops 29491200 | bytes 3328352 | tf_op jit(solution)/shard_map/kfd,fdry->kry/dot_general | solution.py:110
  86.3 34.8 %psum.7 = f32[3,16,256]{2,0,1:T(4,128)S(1)} all-reduce(f32[3,16,256]{2,0,1:T(4,128)S(1)} %convolution_bitcast_fusion), channel_id=1, replica_groups=mesh['pts'=32,'dir'=8] {'dir'}, use_global_device_ids=true, to_apply=%region_0.1 | all-reduce | flops 12288 | bytes 98304 | tf_op jit(solution)/shard_map/psum | solution.py:116
  121.1 1.9 %collective-permute-start.8 = (f32[3,1,256]{2,1,0:T(1,128)S(1)}, f32[3,1,256]{2,1,0:T(1,128)S(1)}, u32[]{:S(2)}, u32[]{:S(2)}) collective-permute-start(f32[3,1,256]{2,1,0:T(1,128)S(1)} %get-tuple-element.20), channel_id=1, source_target_pairs={{8,0},{16,8},{24,16},{32,24},{40,32},{48,40},{56,48},{64,56},{72,6... | collective-permute-start | bytes 9224 | tf_op jit(solution)/shard_map/ppermute | solution.py:16
  123.1 2.4 %collective-permute-start.9 = (f32[3,1,256]{2,1,0:T(1,128)S(1)}, f32[3,1,256]{2,1,0:T(1,128)S(1)}, u32[]{:S(2)}, u32[]{:S(2)}) collective-permute-start(f32[3,1,256]{2,1,0:T(1,128)S(1)} %get-tuple-element.21), channel_id=1, source_target_pairs={{0,8},{8,16},{16,24},{24,32},{32,40},{40,48},{48,56},{56,64},{64,7... | collective-permute-start | bytes 9224 | tf_op jit(solution)/shard_map/ppermute | solution.py:15
  125.5 4.8 %copy.46 = f32[50,4,16,256]{3,2,1,0:T(8,128)} copy(f32[50,4,16,256]{3,0,2,1:T(8,128)} %copy-done.2) | data formatting | bytes 6553600
  130.4 1.2 collective-permute-done.9
  131.6 0.1 fusion.32
  131.7 0.6 pad_maximum_fusion.1
  (33 shorter events, 0.5 us)
Async XLA Ops:
  2.1 25.2 %collective-permute-start = (f32[3,2,256]{2,1,0:T(2,128)S(1)}, f32[3,2,256]{2,1,0:T(2,128)S(1)}, u32[]{:S(2)}, u32[]{:S(2)}) collective-permute-start(f32[3,2,256]{2,1,0:T(2,128)S(1)} %get-tuple-element.24), channel_id=1, source_target_pairs={{0,8},{8,16},{16,24},{24,32},{32,40},{40,48},{48,56},{56,64},{64,7... | collective-permute-start | bytes 18440 | tf_op jit(solution)/shard_map/ppermute | solution.py:15
  4.0 23.3 %collective-permute-start.1 = (f32[3,2,256]{2,1,0:T(2,128)S(1)}, f32[3,2,256]{2,1,0:T(2,128)S(1)}, u32[]{:S(2)}, u32[]{:S(2)}) collective-permute-start(f32[3,2,256]{2,1,0:T(2,128)S(1)} %get-tuple-element.25), channel_id=1, source_target_pairs={{8,0},{16,8},{24,16},{32,24},{40,32},{48,40},{56,48},{64,56},{72,6... | collective-permute-start | bytes 18440 | tf_op jit(solution)/shard_map/ppermute | solution.py:16
  12.1 15.0 %copy-start.5 = (f32[50]{0:T(128)S(1)}, f32[50]{0:T(128)}, u32[]{:S(2)}) copy-start(f32[50]{0:T(128)} %param.10) | copy-start | bytes 604
  12.1 15.0 %copy-start.6 = (f32[50]{0:T(128)S(1)}, f32[50]{0:T(128)}, u32[]{:S(2)}) copy-start(f32[50]{0:T(128)} %param.11) | copy-start | bytes 604
  12.1 15.1 %copy-start.7 = (f32[50]{0:T(128)S(1)}, f32[50]{0:T(128)}, u32[]{:S(2)}) copy-start(f32[50]{0:T(128)} %param.9) | copy-start | bytes 604
  12.1 15.2 %copy-start.4 = (f32[2,16,256]{2,1,0:T(8,128)S(1)}, f32[2,16,256]{2,1,0:T(8,128)}, u32[]{:S(2)}) copy-start(f32[2,16,256]{2,1,0:T(8,128)} %param.7) | copy-start | bytes 98308
  16.0 1.8 %copy-start = (f32[50,4,16,256]{3,0,2,1:T(8,128)}, f32[50,4,16,256]{3,0,2,1:T(8,128)S(1)}, u32[]{:S(2)}) copy-start(f32[50,4,16,256]{3,0,2,1:T(8,128)S(1)} %copy_multiply_fusion) | copy-start | bytes 9830404
  17.8 14.5 %collective-permute-start.2 = (f32[50,4,1,256]{3,0,2,1:T(8,128)S(1)}, f32[50,4,1,256]{3,0,2,1:T(8,128)S(1)}, u32[]{:S(2)}, u32[]{:S(2)}) collective-permute-start(f32[50,4,1,256]{3,0,2,1:T(8,128)S(1)} %get-tuple-element.15), channel_id=1, source_target_pairs={{0,8},{8,16},{16,24},{24,32},{32,40},{40,48},{48,56},{56,64},{64,7... | collective-permute-start | bytes 614408 | tf_op jit(solution)/shard_map/ppermute | solution.py:15
  19.7 12.6 %collective-permute-start.3 = (f32[50,4,1,256]{3,0,2,1:T(8,128)S(1)}, f32[50,4,1,256]{3,0,2,1:T(8,128)S(1)}, u32[]{:S(2)}, u32[]{:S(2)}) collective-permute-start(f32[50,4,1,256]{3,0,2,1:T(8,128)S(1)} %get-tuple-element.14), channel_id=1, source_target_pairs={{8,0},{16,8},{24,16},{32,24},{40,32},{48,40},{56,48},{64,56},{72,6... | collective-permute-start | bytes 614408 | tf_op jit(solution)/shard_map/ppermute | solution.py:16
  27.4 4.9 %copy-start.1 = (f32[50,4,16,256]{3,0,2,1:T(8,128)S(1)}, f32[50,4,16,256]{3,0,2,1:T(8,128)}, u32[]{:S(2)}) copy-start(f32[50,4,16,256]{3,0,2,1:T(8,128)} %copy-done) | copy-start | bytes 9830404
  32.3 1.9 %copy-start.3 = (f32[50,4,16,256]{3,2,1,0:T(8,128)S(1)}, f32[50,4,16,256]{3,2,1,0:T(8,128)}, u32[]{:S(2)}) copy-start(f32[50,4,16,256]{3,2,1,0:T(8,128)} %param.6) | copy-start | bytes 9830404
  39.4 12.5 %collective-permute-start.4 = (f32[50,4,1,256]{3,0,2,1:T(8,128)S(1)}, f32[50,4,1,256]{3,0,2,1:T(8,128)S(1)}, u32[]{:S(2)}, u32[]{:S(2)}) collective-permute-start(f32[50,4,1,256]{3,0,2,1:T(8,128)S(1)} %get-tuple-element.13), channel_id=1, source_target_pairs={{0,8},{8,16},{16,24},{24,32},{32,40},{40,48},{48,56},{56,64},{64,7... | collective-permute-start | bytes 614408 | tf_op jit(solution)/shard_map/ppermute | solution.py:15
  41.3 10.8 %collective-permute-start.5 = (f32[50,4,1,256]{3,0,2,1:T(8,128)S(1)}, f32[50,4,1,256]{3,0,2,1:T(8,128)S(1)}, u32[]{:S(2)}, u32[]{:S(2)}) collective-permute-start(f32[50,4,1,256]{3,0,2,1:T(8,128)S(1)} %get-tuple-element.12), channel_id=1, source_target_pairs={{8,0},{16,8},{24,16},{32,24},{40,32},{48,40},{56,48},{64,56},{72,6... | collective-permute-start | bytes 614408 | tf_op jit(solution)/shard_map/ppermute | solution.py:16
  62.5 17.3 %collective-permute-start.6 = (f32[50,1,16,256]{3,2,1,0:T(8,128)S(1)}, f32[50,1,16,256]{3,2,1,0:T(8,128)S(1)}, u32[]{:S(2)}, u32[]{:S(2)}) collective-permute-start(f32[50,1,16,256]{3,2,1,0:T(8,128)S(1)} %copy.35), channel_id=1, source_target_pairs={{0,1},{1,2},{2,3},{3,4},{4,5},{5,6},{6,7},{7,0},{8,9},{9,10},{10,1... | collective-permute-start | bytes 2457608 | tf_op jit(solution)/shard_map/ppermute | solution.py:15
  64.4 15.9 %collective-permute-start.7 = (f32[50,1,16,256]{3,2,1,0:T(8,128)S(1)}, f32[50,1,16,256]{3,2,1,0:T(8,128)S(1)}, u32[]{:S(2)}, u32[]{:S(2)}) collective-permute-start(f32[50,1,16,256]{3,2,1,0:T(8,128)S(1)} %copy.37), channel_id=1, source_target_pairs={{1,0},{2,1},{3,2},{4,3},{5,4},{6,5},{7,6},{0,7},{9,8},{10,9},{11,1... | collective-permute-start | bytes 2457608 | tf_op jit(solution)/shard_map/ppermute | solution.py:16
  82.6 1.8 %copy-start.2 = (f32[50,4,16,256]{3,0,2,1:T(8,128)}, f32[50,4,16,256]{3,0,2,1:T(8,128)S(1)}, u32[]{:S(2)}) copy-start(f32[50,4,16,256]{3,0,2,1:T(8,128)S(1)} %fusion.13) | copy-start | bytes 9830404
  121.1 9.2 %collective-permute-start.8 = (f32[3,1,256]{2,1,0:T(1,128)S(1)}, f32[3,1,256]{2,1,0:T(1,128)S(1)}, u32[]{:S(2)}, u32[]{:S(2)}) collective-permute-start(f32[3,1,256]{2,1,0:T(1,128)S(1)} %get-tuple-element.20), channel_id=1, source_target_pairs={{8,0},{16,8},{24,16},{32,24},{40,32},{48,40},{56,48},{64,56},{72,6... | collective-permute-start | bytes 9224 | tf_op jit(solution)/shard_map/ppermute | solution.py:16
  123.1 8.5 %collective-permute-start.9 = (f32[3,1,256]{2,1,0:T(1,128)S(1)}, f32[3,1,256]{2,1,0:T(1,128)S(1)}, u32[]{:S(2)}, u32[]{:S(2)}) collective-permute-start(f32[3,1,256]{2,1,0:T(1,128)S(1)} %get-tuple-element.21), channel_id=1, source_target_pairs={{0,8},{8,16},{16,24},{24,32},{32,40},{40,48},{48,56},{56,64},{64,7... | collective-permute-start | bytes 9224 | tf_op jit(solution)/shard_map/ppermute | solution.py:15
where the time goes:
time: 133 us; the launch traced here: 132 us
  starting transfers between devices  37.1 us (28%)
  blocking collectives  34.8 us (26%)
  other arithmetic  32.9 us (25%)
  waiting for transfers between devices  13.6 us (10%)
  local copies, waits for them, and re-layouts  10.9 us (8%)
  matrix products  1.93 us (1%)
    psum x1, blocking collectives, per_device(): summed = lax.psum(partial_value, 'dir')  34.8 us
    ppermute x5, starting transfers between devices, with_halo(): after = lax.ppermute(first, axis, down)  27.3 us
    ppermute x5, waiting for transfers between devices, with_halo(): before = lax.ppermute(last, axis, up)  13.4 us
    add x5, other arithmetic, upwind(): jnp.maximum(velocity, 0.0) * behind + jnp.minimum(velocity, 0.0) * in_front  13 us
    mul x2, other arithmetic, advance(): return land_cells * (middle - change)  12.6 us
    ppermute x5, starting transfers between devices, with_halo(): before = lax.ppermute(last, axis, up)  9.81 us
    unnamed x19, local copies, waits for them, and re-layouts  9.12 us
    mul x1, other arithmetic, per_device(): spectra = land_cells * action  3.85 us
  transfers between devices with their start and end apart: 10, of which 3 were waited for; matrix products, arithmetic and copies ran while one was open for 14% of the time, Pallas kernels for 0%

commit v1 on v0

--- a/solution.py
+++ b/solution.py
@@ -113,7 +113,8 @@
         new_action,
         precision=lax.Precision.HIGHEST,
     )
-    summed = lax.psum(partial_value, "dir")
+    parts = lax.all_gather(partial_value, "dir")
+    summed = jnp.sum(parts, axis=0)
     extended = with_halo(summed, (("pts", 1),), 1, False)
     return (new_action, wave_force_of(extended))
 

time: 133 us -> 127 us (0.955)
  blocking collectives: 34.8 us -> 28.6 us
    psum x1 -> x0, blocking collectives: 34.8 us -> none  [per_device(): summed = lax.psum(partial_value, 'dir')]
    all_gather x0 -> x1, blocking collectives: none -> 28.6 us  [per_device(): parts = lax.all_gather(partial_value, 'dir')]
    unnamed x19 -> x17, local copies, waits for them, and re-layouts: 9.12 us -> 9.11 us
  transfers between devices with their start and end apart: 10 -> 10, of which waited for: 3 -> 3; matrix products, arithmetic and copies ran while one was open for 14% -> 15% of each run, Pallas kernels for 0% -> 0%
where the time goes in v1:
time: 127 us; the launch traced here: 126 us
  starting transfers between devices  37.1 us (29%)
  other arithmetic  33 us (26%)
  blocking collectives  28.6 us (23%)
  waiting for transfers between devices  13.7 us (11%)
  local copies, waits for them, and re-layouts  10.8 us (9%)
  matrix products  1.93 us (2%)
    all_gather x1, blocking collectives, per_device(): parts = lax.all_gather(partial_value, 'dir')  28.6 us
    ppermute x5, starting transfers between devices, with_halo(): after = lax.ppermute(first, axis, down)  27.3 us
    ppermute x5, waiting for transfers between devices, with_halo(): before = lax.ppermute(last, axis, up)  13.5 us
    add x5, other arithmetic, upwind(): jnp.maximum(velocity, 0.0) * behind + jnp.minimum(velocity, 0.0) * in_front  13 us
    mul x2, other arithmetic, advance(): return land_cells * (middle - change)  12.6 us
    ppermute x5, starting transfers between devices, with_halo(): before = lax.ppermute(last, axis, up)  9.81 us
    unnamed x17, local copies, waits for them, and re-layouts  9.11 us
    mul x1, other arithmetic, per_device(): spectra = land_cells * action  3.85 us
  transfers between devices with their start and end apart: 10, of which 3 were waited for; matrix products, arithmetic and copies ran while one was open for 15% of the time, Pallas kernels for 0%

profile of v1, /device:TPU:6, one launch (start us, length us, event | category | flops | bytes accessed | tf_op | source)
XLA Modules:
  0.0 126.1 jit_solution(16522288837843516729)
XLA Ops:
  0.6 0.7 convert_bitcast_fusion
  1.4 0.7 pad_maximum_fusion.5
  2.1 1.9 %collective-permute-start = (f32[3,2,256]{2,1,0:T(2,128)S(1)}, f32[3,2,256]{2,1,0:T(2,128)S(1)}, u32[]{:S(2)}, u32[]{:S(2)}) collective-permute-start(f32[3,2,256]{2,1,0:T(2,128)S(1)} %get-tuple-element.24), channel_id=1, source_target_pairs={{0,8},{8,16},{16,24},{24,32},{32,40},{40,48},{48,56},{56,64},{64,7... | collective-permute-start | bytes 18440 | tf_op jit(solution)/shard_map/ppermute | solution.py:15
  4.0 8.0 %collective-permute-start.1 = (f32[3,2,256]{2,1,0:T(2,128)S(1)}, f32[3,2,256]{2,1,0:T(2,128)S(1)}, u32[]{:S(2)}, u32[]{:S(2)}) collective-permute-start(f32[3,2,256]{2,1,0:T(2,128)S(1)} %get-tuple-element.25), channel_id=1, source_target_pairs={{8,0},{16,8},{24,16},{32,24},{40,32},{48,40},{56,48},{64,56},{72,6... | collective-permute-start | bytes 18440 | tf_op jit(solution)/shard_map/ppermute | solution.py:16
  12.1 0.0 copy-start.5
  12.1 0.0 copy-start.6
  12.1 0.0 copy-start.7
  12.1 0.0 copy-start.4
  12.1 3.9 %copy_multiply_fusion = f32[50,4,16,256]{3,0,2,1:T(8,128)S(1)} fusion(f32[50,4,16,256]{3,2,1,0:T(8,128)} %param.6, f32[16,256]{1,0:T(8,128)S(1)} %get-tuple-element.30), kind=kLoop, calls=%fused_computation.35 | loop fusion | flops 819200 | bytes 6569984 | tf_op jit(solution)/shard_map/mul | solution.py:101
  16.0 1.8 %copy-done = f32[50,4,16,256]{3,0,2,1:T(8,128)} copy-done((f32[50,4,16,256]{3,0,2,1:T(8,128)}, f32[50,4,16,256]{3,0,2,1:T(8,128)S(1)}, u32[]{:S(2)}) %copy-start) | copy-done | bytes 3276824
  17.8 1.9 %collective-permute-start.2 = (f32[50,4,1,256]{3,0,2,1:T(8,128)S(1)}, f32[50,4,1,256]{3,0,2,1:T(8,128)S(1)}, u32[]{:S(2)}, u32[]{:S(2)}) collective-permute-start(f32[50,4,1,256]{3,0,2,1:T(8,128)S(1)} %get-tuple-element.13), channel_id=1, source_target_pairs={{0,8},{8,16},{16,24},{24,32},{32,40},{40,48},{48,56},{56,64},{64,7... | collective-permute-start | bytes 614408 | tf_op jit(solution)/shard_map/ppermute | solution.py:15
  19.7 7.3 %collective-permute-start.3 = (f32[50,4,1,256]{3,0,2,1:T(8,128)S(1)}, f32[50,4,1,256]{3,0,2,1:T(8,128)S(1)}, u32[]{:S(2)}, u32[]{:S(2)}) collective-permute-start(f32[50,4,1,256]{3,0,2,1:T(8,128)S(1)} %get-tuple-element.12), channel_id=1, source_target_pairs={{8,0},{16,8},{24,16},{32,24},{40,32},{48,40},{56,48},{64,56},{72,6... | collective-permute-start | bytes 614408 | tf_op jit(solution)/shard_map/ppermute | solution.py:16
  27.1 0.1 broadcast_multiply_fusion
  27.2 0.1 broadcast_multiply_fusion.2
  27.4 0.1 fusion.23
  27.4 4.8 %fusion.4 = f32[50,4,16,257]{3,0,2,1:T(8,128)S(1)} fusion(f32[50,4,16,256]{3,0,2,1:T(8,128)} %copy-done, f32[16,257]{1,0:T(8,128)S(1)} %fusion.23, f32[50,4]{0,1:T(4,128)S(1)} %get-tuple-element.34), kind=kLoop, calls=%fused_computation.12 | loop fusion | flops 4934400 | bytes 6583648 | tf_op jit(solution)/shard_map/add | solution.py:22
  32.3 0.0 copy-start.3
  32.3 1.2 fusion.11
  33.5 0.7 copy-done.3
  34.2 5.1 %fusion.19 = f32[50,4,16,256]{3,0,2,1:T(8,128)S(1)} fusion(f32[50,4,16,257]{3,0,2,1:T(8,128)S(1)} %fusion.4, f32[50,4,17,256]{3,0,2,1:T(8,128)S(1)} %fusion.11, f32[16,256]{1,0:T(8,128)S(1)} %get-tuple-element.30, f32[50,4,16,256]{3,2,1,0:T(8,128)S(1)} %copy-done.3), kind=kLoop, calls=%fused_computation.33 | loop fusion | flops 4915200 | bytes 19677184 | tf_op jit(solution)/shard_map/mul | solution.py:36
  39.4 1.9 %collective-permute-start.4 = (f32[50,4,1,256]{3,0,2,1:T(8,128)S(1)}, f32[50,4,1,256]{3,0,2,1:T(8,128)S(1)}, u32[]{:S(2)}, u32[]{:S(2)}) collective-permute-start(f32[50,4,1,256]{3,0,2,1:T(8,128)S(1)} %get-tuple-element.11), channel_id=1, source_target_pairs={{0,8},{8,16},{16,24},{24,32},{32,40},{40,48},{48,56},{56,64},{64,7... | collective-permute-start | bytes 614408 | tf_op jit(solution)/shard_map/ppermute | solution.py:15
  41.3 7.3 %collective-permute-start.5 = (f32[50,4,1,256]{3,0,2,1:T(8,128)S(1)}, f32[50,4,1,256]{3,0,2,1:T(8,128)S(1)}, u32[]{:S(2)}, u32[]{:S(2)}) collective-permute-start(f32[50,4,1,256]{3,0,2,1:T(8,128)S(1)} %get-tuple-element.10), channel_id=1, source_target_pairs={{8,0},{16,8},{24,16},{32,24},{40,32},{48,40},{56,48},{64,56},{72,6... | collective-permute-start | bytes 614408 | tf_op jit(solution)/shard_map/ppermute | solution.py:16
  48.6 3.3 %fusion.5 = f32[50,4,16,257]{3,0,2,1:T(8,128)} fusion(f32[50,4,16,256]{3,0,2,1:T(8,128)S(1)} %fusion.19, f32[16,257]{1,0:T(8,128)S(1)} %fusion.23, f32[50,4]{0,1:T(4,128)S(1)} %get-tuple-element.34), kind=kLoop, calls=%fused_computation.13 | loop fusion | flops 4934400 | bytes 6583648 | tf_op jit(solution)/shard_map/add | solution.py:22
  51.9 0.2 collective-permute-done.5
  52.1 2.5 %fusion.12 = f32[50,4,17,256]{3,0,2,1:T(8,128)} fusion(f32[50,4,16,256]{3,0,2,1:T(8,128)S(1)} %fusion.19, f32[50,4,1,256]{3,0,2,1:T(8,128)S(1)} %collective-permute-done.4, f32[50,4,1,256]{3,0,2,1:T(8,128)S(1)} %collective-permute-done.5, f32[17,256]{1,0:T(8,128)S(1)} %fusion.25, f32[50,4]{0,1:T(4,128)S(1)} %get-tuple-element.33), kind=kLoop, calls=%fused_computation.22 | loop fusion | flops 6963200 | bytes 7186208 | tf_op jit(solution)/shard_map/add | solution.py:22
  54.6 7.5 %fusion.16 = f32[50,4,16,256]{3,0,2,1:T(8,128)S(1)} fusion(f32[50,4,16,256]{3,0,2,1:T(8,128)S(1)} %fusion.19, f32[50,4,16,257]{3,0,2,1:T(8,128)} %fusion.5, f32[50,4,17,256]{3,0,2,1:T(8,128)} %fusion.12, f32[16,256]{1,0:T(8,128)S(1)} %get-tuple-element.30), kind=kLoop, calls=%fused_computation.28 | loop fusion | flops 4096000 | bytes 19677184 | tf_op jit(solution)/shard_map/mul | solution.py:36
  62.1 0.1 fusion.58
  62.2 0.3 copy.24
  62.5 1.7 %collective-permute-start.6 = (f32[50,1,16,256]{3,2,1,0:T(8,128)S(1)}, f32[50,1,16,256]{3,2,1,0:T(8,128)S(1)}, u32[]{:S(2)}, u32[]{:S(2)}) collective-permute-start(f32[50,1,16,256]{3,2,1,0:T(8,128)S(1)} %copy.24), channel_id=1, source_target_pairs={{0,1},{1,2},{2,3},{3,4},{4,5},{5,6},{6,7},{7,0},{8,9},{9,10},{10,1... | collective-permute-start | bytes 2457608 | tf_op jit(solution)/shard_map/ppermute | solution.py:15
  64.1 0.3 copy.26
  64.4 2.8 %collective-permute-start.7 = (f32[50,1,16,256]{3,2,1,0:T(8,128)S(1)}, f32[50,1,16,256]{3,2,1,0:T(8,128)S(1)}, u32[]{:S(2)}, u32[]{:S(2)}) collective-permute-start(f32[50,1,16,256]{3,2,1,0:T(8,128)S(1)} %copy.26), channel_id=1, source_target_pairs={{1,0},{2,1},{3,2},{4,3},{5,4},{6,5},{7,6},{0,7},{9,8},{10,9},{11,1... | collective-permute-start | bytes 2457608 | tf_op jit(solution)/shard_map/ppermute | solution.py:16
  67.3 0.1 add_multiply_fusion.1
  67.4 0.1 fusion.27
  67.5 0.1 fusion.21
  67.6 12.2 %collective-permute-done.6 = f32[50,1,16,256]{3,2,1,0:T(8,128)S(1)} collective-permute-done((f32[50,1,16,256]{3,2,1,0:T(8,128)S(1)}, f32[50,1,16,256]{3,2,1,0:T(8,128)S(1)}, u32[]{:S(2)}, u32[]{:S(2)}) %collective-permute-start.6) | collective-permute-done | bytes 819232 | tf_op jit(solution)/shard_map/ppermute | solution.py:15
  79.8 0.5 copy.25
  80.3 0.5 copy.27
  80.8 1.1 fusion.10
  81.9 0.6 fusion.13
  82.6 1.8 %copy-done.2 = f32[50,4,16,256]{3,0,2,1:T(8,128)} copy-done((f32[50,4,16,256]{3,0,2,1:T(8,128)}, f32[50,4,16,256]{3,0,2,1:T(8,128)S(1)}, u32[]{:S(2)}) %copy-start.2) | copy-done | bytes 3276824
  84.4 1.9 %convolution_bitcast_fusion = f32[3,16,256]{2,0,1:T(4,128)S(1)} fusion(f32[50,4,16,256]{3,0,2,1:T(8,128)S(1)} %fusion.13, f32[3,50,4]{1,2,0:T(4,128)S(1)} %pad_maximum_fusion.6), kind=kOutput, calls=%fused_computation.36 | convolution fusion | flops 29491200 | bytes 3328352 | tf_op jit(solution)/shard_map/kfd,fdry->kry/dot_general | solution.py:110
  86.3 28.6 %all-gather = f32[24,16,256]{2,1,0:T(8,128)S(1)} all-gather(f32[3,16,256]{2,1,0:T(8,128)S(1)} %copy.30), channel_id=2, replica_groups=mesh['pts'=32,'dir'=8] {'dir'}, dimensions={0}, use_global_device_ids=true | all-gather | bytes 442368 | tf_op jit(solution)/shard_map/all_gather | solution.py:116
  115.0 1.9 %collective-permute-start.8 = (f32[3,1,256]{2,1,0:T(1,128)S(1)}, f32[3,1,256]{2,1,0:T(1,128)S(1)}, u32[]{:S(2)}, u32[]{:S(2)}) collective-permute-start(f32[3,1,256]{2,1,0:T(1,128)S(1)} %get-tuple-element.20), channel_id=1, source_target_pairs={{8,0},{16,8},{24,16},{32,24},{40,32},{48,40},{56,48},{64,56},{72,6... | collective-permute-start | bytes 9224 | tf_op jit(solution)/shard_map/ppermute | solution.py:16
  116.9 2.4 %collective-permute-start.9 = (f32[3,1,256]{2,1,0:T(1,128)S(1)}, f32[3,1,256]{2,1,0:T(1,128)S(1)}, u32[]{:S(2)}, u32[]{:S(2)}) collective-permute-start(f32[3,1,256]{2,1,0:T(1,128)S(1)} %get-tuple-element.21), channel_id=1, source_target_pairs={{0,8},{8,16},{16,24},{24,32},{32,40},{40,48},{48,56},{56,64},{64,7... | collective-permute-start | bytes 9224 | tf_op jit(solution)/shard_map/ppermute | solution.py:15
  119.3 4.8 %copy.31 = f32[50,4,16,256]{3,2,1,0:T(8,128)} copy(f32[50,4,16,256]{3,0,2,1:T(8,128)} %copy-done.2) | data formatting | bytes 6553600
  124.1 1.3 %collective-permute-done.9 = f32[3,1,256]{2,1,0:T(1,128)S(1)} collective-permute-done((f32[3,1,256]{2,1,0:T(1,128)S(1)}, f32[3,1,256]{2,1,0:T(1,128)S(1)}, u32[]{:S(2)}, u32[]{:S(2)}) %collective-permute-start.9) | collective-permute-done | bytes 3104 | tf_op jit(solution)/shard_map/ppermute | solution.py:15
  125.4 0.1 fusion.32
  125.5 0.6 pad_maximum_fusion.1
  (31 shorter events, 0.4 us)
Async XLA Ops:
  2.1 25.2 %collective-permute-start = (f32[3,2,256]{2,1,0:T(2,128)S(1)}, f32[3,2,256]{2,1,0:T(2,128)S(1)}, u32[]{:S(2)}, u32[]{:S(2)}) collective-permute-start(f32[3,2,256]{2,1,0:T(2,128)S(1)} %get-tuple-element.24), channel_id=1, source_target_pairs={{0,8},{8,16},{16,24},{24,32},{32,40},{40,48},{48,56},{56,64},{64,7... | collective-permute-start | bytes 18440 | tf_op jit(solution)/shard_map/ppermute | solution.py:15
  4.0 23.3 %collective-permute-start.1 = (f32[3,2,256]{2,1,0:T(2,128)S(1)}, f32[3,2,256]{2,1,0:T(2,128)S(1)}, u32[]{:S(2)}, u32[]{:S(2)}) collective-permute-start(f32[3,2,256]{2,1,0:T(2,128)S(1)} %get-tuple-element.25), channel_id=1, source_target_pairs={{8,0},{16,8},{24,16},{32,24},{40,32},{48,40},{56,48},{64,56},{72,6... | collective-permute-start | bytes 18440 | tf_op jit(solution)/shard_map/ppermute | solution.py:16
  12.1 15.0 %copy-start.5 = (f32[50]{0:T(128)S(1)}, f32[50]{0:T(128)}, u32[]{:S(2)}) copy-start(f32[50]{0:T(128)} %param.10) | copy-start | bytes 604
  12.1 15.0 %copy-start.6 = (f32[50]{0:T(128)S(1)}, f32[50]{0:T(128)}, u32[]{:S(2)}) copy-start(f32[50]{0:T(128)} %param.11) | copy-start | bytes 604
  12.1 15.1 %copy-start.7 = (f32[50]{0:T(128)S(1)}, f32[50]{0:T(128)}, u32[]{:S(2)}) copy-start(f32[50]{0:T(128)} %param.9) | copy-start | bytes 604
  12.1 15.2 %copy-start.4 = (f32[2,16,256]{2,1,0:T(8,128)S(1)}, f32[2,16,256]{2,1,0:T(8,128)}, u32[]{:S(2)}) copy-start(f32[2,16,256]{2,1,0:T(8,128)} %param.7) | copy-start | bytes 98308
  16.0 1.8 %copy-start = (f32[50,4,16,256]{3,0,2,1:T(8,128)}, f32[50,4,16,256]{3,0,2,1:T(8,128)S(1)}, u32[]{:S(2)}) copy-start(f32[50,4,16,256]{3,0,2,1:T(8,128)S(1)} %copy_multiply_fusion) | copy-start | bytes 9830404
  17.8 14.5 %collective-permute-start.2 = (f32[50,4,1,256]{3,0,2,1:T(8,128)S(1)}, f32[50,4,1,256]{3,0,2,1:T(8,128)S(1)}, u32[]{:S(2)}, u32[]{:S(2)}) collective-permute-start(f32[50,4,1,256]{3,0,2,1:T(8,128)S(1)} %get-tuple-element.13), channel_id=1, source_target_pairs={{0,8},{8,16},{16,24},{24,32},{32,40},{40,48},{48,56},{56,64},{64,7... | collective-permute-start | bytes 614408 | tf_op jit(solution)/shard_map/ppermute | solution.py:15
  19.7 12.6 %collective-permute-start.3 = (f32[50,4,1,256]{3,0,2,1:T(8,128)S(1)}, f32[50,4,1,256]{3,0,2,1:T(8,128)S(1)}, u32[]{:S(2)}, u32[]{:S(2)}) collective-permute-start(f32[50,4,1,256]{3,0,2,1:T(8,128)S(1)} %get-tuple-element.12), channel_id=1, source_target_pairs={{8,0},{16,8},{24,16},{32,24},{40,32},{48,40},{56,48},{64,56},{72,6... | collective-permute-start | bytes 614408 | tf_op jit(solution)/shard_map/ppermute | solution.py:16
  27.4 4.9 %copy-start.1 = (f32[50,4,16,256]{3,0,2,1:T(8,128)S(1)}, f32[50,4,16,256]{3,0,2,1:T(8,128)}, u32[]{:S(2)}) copy-start(f32[50,4,16,256]{3,0,2,1:T(8,128)} %copy-done) | copy-start | bytes 9830404
  32.3 1.9 %copy-start.3 = (f32[50,4,16,256]{3,2,1,0:T(8,128)S(1)}, f32[50,4,16,256]{3,2,1,0:T(8,128)}, u32[]{:S(2)}) copy-start(f32[50,4,16,256]{3,2,1,0:T(8,128)} %param.6) | copy-start | bytes 9830404
  39.4 12.5 %collective-permute-start.4 = (f32[50,4,1,256]{3,0,2,1:T(8,128)S(1)}, f32[50,4,1,256]{3,0,2,1:T(8,128)S(1)}, u32[]{:S(2)}, u32[]{:S(2)}) collective-permute-start(f32[50,4,1,256]{3,0,2,1:T(8,128)S(1)} %get-tuple-element.11), channel_id=1, source_target_pairs={{0,8},{8,16},{16,24},{24,32},{32,40},{40,48},{48,56},{56,64},{64,7... | collective-permute-start | bytes 614408 | tf_op jit(solution)/shard_map/ppermute | solution.py:15
  41.3 10.8 %collective-permute-start.5 = (f32[50,4,1,256]{3,0,2,1:T(8,128)S(1)}, f32[50,4,1,256]{3,0,2,1:T(8,128)S(1)}, u32[]{:S(2)}, u32[]{:S(2)}) collective-permute-start(f32[50,4,1,256]{3,0,2,1:T(8,128)S(1)} %get-tuple-element.10), channel_id=1, source_target_pairs={{8,0},{16,8},{24,16},{32,24},{40,32},{48,40},{56,48},{64,56},{72,6... | collective-permute-start | bytes 614408 | tf_op jit(solution)/shard_map/ppermute | solution.py:16
  62.5 17.3 %collective-permute-start.6 = (f32[50,1,16,256]{3,2,1,0:T(8,128)S(1)}, f32[50,1,16,256]{3,2,1,0:T(8,128)S(1)}, u32[]{:S(2)}, u32[]{:S(2)}) collective-permute-start(f32[50,1,16,256]{3,2,1,0:T(8,128)S(1)} %copy.24), channel_id=1, source_target_pairs={{0,1},{1,2},{2,3},{3,4},{4,5},{5,6},{6,7},{7,0},{8,9},{9,10},{10,1... | collective-permute-start | bytes 2457608 | tf_op jit(solution)/shard_map/ppermute | solution.py:15
  64.4 15.9 %collective-permute-start.7 = (f32[50,1,16,256]{3,2,1,0:T(8,128)S(1)}, f32[50,1,16,256]{3,2,1,0:T(8,128)S(1)}, u32[]{:S(2)}, u32[]{:S(2)}) collective-permute-start(f32[50,1,16,256]{3,2,1,0:T(8,128)S(1)} %copy.26), channel_id=1, source_target_pairs={{1,0},{2,1},{3,2},{4,3},{5,4},{6,5},{7,6},{0,7},{9,8},{10,9},{11,1... | collective-permute-start | bytes 2457608 | tf_op jit(solution)/shard_map/ppermute | solution.py:16
  82.6 1.8 %copy-start.2 = (f32[50,4,16,256]{3,0,2,1:T(8,128)}, f32[50,4,16,256]{3,0,2,1:T(8,128)S(1)}, u32[]{:S(2)}) copy-start(f32[50,4,16,256]{3,0,2,1:T(8,128)S(1)} %fusion.13) | copy-start | bytes 9830404
  115.0 9.2 %collective-permute-start.8 = (f32[3,1,256]{2,1,0:T(1,128)S(1)}, f32[3,1,256]{2,1,0:T(1,128)S(1)}, u32[]{:S(2)}, u32[]{:S(2)}) collective-permute-start(f32[3,1,256]{2,1,0:T(1,128)S(1)} %get-tuple-element.20), channel_id=1, source_target_pairs={{8,0},{16,8},{24,16},{32,24},{40,32},{48,40},{56,48},{64,56},{72,6... | collective-permute-start | bytes 9224 | tf_op jit(solution)/shard_map/ppermute | solution.py:16
  116.9 8.5 %collective-permute-start.9 = (f32[3,1,256]{2,1,0:T(1,128)S(1)}, f32[3,1,256]{2,1,0:T(1,128)S(1)}, u32[]{:S(2)}, u32[]{:S(2)}) collective-permute-start(f32[3,1,256]{2,1,0:T(1,128)S(1)} %get-tuple-element.21), channel_id=1, source_target_pairs={{0,8},{8,16},{16,24},{24,32},{32,40},{40,48},{48,56},{56,64},{64,7... | collective-permute-start | bytes 9224 | tf_op jit(solution)/shard_map/ppermute | solution.py:15
